TPU v7x, 128 devices: a whole 4x4x4 slice. The times are simulated.
128 devices in a mesh: ex: 16 (over z, y), ey: 8 (over x, core).
Axes of the slice: x: 4, y: 4, z: 4, core: 2. Of those that a mesh axis runs over, the one named last changes fastest.
Arguments:
- tokens: bfloat16 [32768, 768], P(('ex', 'ey')), may hold values from -6 to 6
- routes: int32 [32768, 1], P(('ex', 'ey')), may hold values from 0 to 127; in each aligned block of 256 rows (0 to 255, 256 to 511, ...) at most 4 rows name the same one
- sub_expert: int32 [32768], P(('ex', 'ey')), may hold values from 0 to 1
- probability: float32 [32768], P(('ex', 'ey')), may hold values from 0.2 to 1
- weight_in: bfloat16 [256, 768, 3072], P(('ex', 'ey')), may hold values from -0.21875 to 0.21875
- weight_out: bfloat16 [256, 3072, 768], P(('ex', 'ey')), may hold values from -0.109375 to 0.109375
Outputs:
- mixed: bfloat16 [32768, 768], P(('ex', 'ey'))
Inputs may be any that keep to these rules, and one draw needn't show every extreme that they name: `routes`: among the 256 tokens of one device (aligned blocks of rows), no value is named by more than 4 tokens, a bound that some block reaches.
All inputs are finite; a program needn't handle non-finite values.
Results may differ from a plain program's by a relative error of at most 0.0058.
Values may be sent and summed in bfloat16 or wider, within the bound.
A program may use at most 64 MiB of HBM per device.

v0:
```python
import jax
import jax.numpy as jnp
from jax import lax
from jax.sharding import PartitionSpec as P


def local(tokens, routes, sub_expert, probability, weight_in, weight_out):
    count_ex = lax.axis_size("ex")
    count_ey = lax.axis_size("ey")
    devices_all = count_ex * count_ey
    local_experts = weight_in.shape[0]
    tok_rows = tokens.shape[0]
    width = tokens.shape[1]
    capacity = 2 * tok_rows // devices_all
    owner = routes[:, 0]
    label_key = owner * local_experts + sub_expert
    groups = local_experts * devices_all
    onehot = (label_key[:, None] == jnp.arange(groups, dtype=jnp.int32)[None, :]).astype(
        jnp.bfloat16
    )
    positions = jnp.arange(tok_rows, dtype=jnp.int32)
    earlier = (positions[:, None] > positions[None, :]).astype(jnp.bfloat16)
    before = jnp.dot(earlier, onehot, preferred_element_type=jnp.float32)
    slot = jnp.sum(before * onehot.astype(jnp.float32), axis=1).astype(jnp.int32)
    target = sub_expert * (devices_all * capacity) + owner * capacity + slot
    buffer_rows = jnp.arange(groups * capacity, dtype=jnp.int32)
    placing = (buffer_rows[:, None] == target[None, :]).astype(jnp.bfloat16)
    outgoing = jnp.dot(placing, tokens, preferred_element_type=jnp.float32).astype(jnp.bfloat16)
    arrive_rows = devices_all * capacity
    labels = jnp.full((groups * capacity,), local_experts, jnp.int32).at[target].set(sub_expert)
    shaped = outgoing.reshape(local_experts, devices_all, capacity, width)
    label_shaped = labels.reshape(local_experts, devices_all, capacity)
    arrived, labels_in = (
        lax.all_to_all(shaped, ("ex", "ey"), split_axis=1, concat_axis=1, tiled=True),
        lax.all_to_all(label_shaped, ("ex", "ey"), split_axis=1, concat_axis=1, tiled=True),
    )
    batch = arrived.reshape(local_experts, arrive_rows, width)
    hidden = jax.nn.relu(
        jnp.einsum("lrd,ldf->lrf", batch, weight_in, preferred_element_type=jnp.float32)
    ).astype(jnp.bfloat16)
    result = jnp.einsum(
        "lrf,lfd->lrd", hidden, weight_out, preferred_element_type=jnp.float32
    ).astype(jnp.bfloat16)
    shaped_back = result.reshape(local_experts, devices_all, capacity, width)
    returned = lax.all_to_all(shaped_back, ("ex", "ey"), split_axis=1, concat_axis=1, tiled=True)
    back_rows = returned.reshape(groups * capacity, width)
    gathered = jnp.einsum("rt,rd->td", placing, back_rows, preferred_element_type=jnp.float32)
    return (gathered * probability[:, None]).astype(jnp.bfloat16)


def solution(mesh):
    return jax.shard_map(
        local,
        mesh=mesh,
        in_specs=(
            P(("ex", "ey"), None),
            P(("ex", "ey"), None),
            P(("ex", "ey")),
            P(("ex", "ey")),
            P(("ex", "ey"), None, None),
            P(("ex", "ey"), None, None),
        ),
        out_specs=P(("ex", "ey"), None),
        check_vma=False,
    )
```

profile of v0, /device:TPU:1, one launch (start us, length us, event | category | flops | bytes accessed | tf_op | source)
XLA Modules:
  0.0 84.4 jit_solution(5231021807757352854)
XLA Ops:
  0.0 0.0 copy-start
  0.0 0.7 broadcast_multiply_fusion.1
  0.7 0.7 add.10
  1.4 0.3 fusion.2
  1.7 0.7 convert_add_fusion
  2.4 0.0 copy-done
  2.4 0.6 convolution_convert_fusion.1
  3.0 0.4 reshape.19
  3.4 0.0 copy-start.1
  3.4 0.5 copy.9
  3.9 36.2 %all_to_all.10 = bf16[2,128,4,768]{3,2,0,1:T(4,128)(2,1)S(1)} all-to-all(bf16[2,128,4,768]{3,2,0,1:T(4,128)(2,1)S(1)} %copy.9), channel_id=1, replica_groups=mesh['ex'=16,'ey'=8] {'ex','ey'}, dimensions={1} | all-to-all | bytes 3145728 | tf_op jit(solution)/shard_map/all_to_all | solution.py:34
  40.2 0.0 slice-start
  40.2 1.2 %copy.10 = bf16[2,128,4,768]{3,0,2,1:T(2,128)(2,1)S(1)} copy(bf16[2,128,4,768]{3,2,0,1:T(4,128)(2,1)S(1)} %all_to_all.10) | data formatting | bytes 3145728 | tf_op jit(solution)/shard_map/all_to_all | solution.py:34
  41.4 0.0 copy-done.1
  41.4 0.0 slice-start.1
  41.4 0.0 slice-start.2
  41.4 5.3 %maximum_convert_fusion = bf16[2,512,3072]{2,1,0:T(8,128)(2,1)S(1)} fusion(bf16[2,768,3072]{2,1,0:T(8,128)(2,1)S(1)} %copy-done.1, bf16[2,512,768]{2,0,1:T(2,128)(2,1)S(1)} %bitcast.8), kind=kOutput, calls=%fused_computation | convolution fusion | flops 4838129664 | bytes 17301504 | tf_op jit(solution)/shard_map/lrd,ldf->lrf/dot_general | solution.py:39
  46.8 0.0 slice-done
  46.8 0.0 slice-done.1
  46.8 0.0 slice-done.2
  46.8 5.1 %convolution_convert_fusion = bf16[2,512,768]{2,1,0:T(8,128)(2,1)S(1)} fusion(bf16[2,512,3072]{2,1,0:T(8,128)(2,1)S(1)} %maximum_convert_fusion, bf16[2,3072,768]{2,1,0:T(8,128)(2,1)S(1)} %bitcast.12), kind=kOutput, calls=%fused_computation.1 | convolution fusion | flops 4832624640 | bytes 17301504 | tf_op jit(solution)/shard_map/lrf,lfd->lrd/dot_general | solution.py:41
  51.9 0.4 reshape.21
  52.3 0.5 copy.12
  52.9 28.9 %all_to_all.11 = bf16[2,128,4,768]{3,2,0,1:T(4,128)(2,1)S(1)} all-to-all(bf16[2,128,4,768]{3,2,0,1:T(4,128)(2,1)S(1)} %copy.12), channel_id=1, replica_groups=mesh['ex'=16,'ey'=8] {'ex','ey'}, dimensions={1} | all-to-all | bytes 3145728 | tf_op jit(solution)/shard_map/all_to_all | solution.py:45
  81.8 0.5 copy.13
  82.3 0.0 copy-start.2
  82.3 0.4 reshape.22
  82.7 0.3 copy-done.2
  83.0 1.4 %fusion.1 = bf16[256,768]{1,0:T(8,128)(2,1)} fusion(bf16[1024,768]{1,0:T(8,128)(2,1)S(1)} %reshape.22, s32[256]{0:T(256)S(1)} %convert_add_fusion, f32[256]{0:T(256)S(1)} %copy-done.2), kind=kOutput, calls=%fused_computation.5 | convolution fusion | flops 403308544 | bytes 1968128 | tf_op jit(solution)/shard_map/rt,rd->td/dot_general | solution.py:47
  (1 shorter events, 0.0 us)
Async XLA Ops:
  0.0 2.4 %copy-start = (bf16[256,768]{1,0:T(8,128)(2,1)S(1)}, bf16[256,768]{1,0:T(8,128)(2,1)}, u32[]{:S(2)}) copy-start(bf16[256,768]{1,0:T(8,128)(2,1)} %param.6) | copy-start | bytes 1179652
  3.4 38.0 %copy-start.1 = (bf16[2,768,3072]{2,1,0:T(8,128)(2,1)S(1)}, bf16[2,768,3072]{2,1,0:T(8,128)(2,1)}, u32[]{:S(2)}) copy-start(bf16[2,768,3072]{2,1,0:T(8,128)(2,1)} %param.10) | copy-start | bytes 28311556
  40.2 6.6 %slice-start = ((s8[9437184]{0:T(1024)(128)(4,1)}), s8[4194304]{0:T(1024)(128)(4,1)S(1)}, s32[]{:S(2)}) async-start(s8[9437184]{0:T(1024)(128)(4,1)} %bitcast.11), calls=%async_computation.2 | async-start | bytes 8388608
  41.4 5.4 %slice-start.1 = ((s8[9437184]{0:T(1024)(128)(4,1)}), s8[4194304]{0:T(1024)(128)(4,1)S(1)}, s32[]{:S(2)}) async-start(s8[9437184]{0:T(1024)(128)(4,1)} %bitcast.11), calls=%async_computation.3 | async-start | bytes 8388608
  41.4 5.4 %slice-start.2 = ((s8[9437184]{0:T(1024)(128)(4,1)}), s8[1048576]{0:T(1024)(128)(4,1)S(1)}, s32[]{:S(2)}) async-start(s8[9437184]{0:T(1024)(128)(4,1)} %bitcast.11), calls=%async_computation.4 | async-start | bytes 2097152
  82.3 0.7 copy-start.2
where the time goes:
time: 84.6 us; the launch traced here: 84.4 us
  blocking collectives  65.1 us (77%)
  matrix products  12.7 us (15%)
  local copies, waits for them, and re-layouts  4.36 us (5%)
  other arithmetic  2.1 us (2%)
    all_to_all x1, blocking collectives, local(): lax.all_to_all(shaped, ('ex', 'ey'), split_axis=1, concat_axis=1, tiled=T...  36.2 us
    all_to_all x1, blocking collectives, local(): lax.all_to_all(shaped_back, ('ex', 'ey'), split_axis=1, concat_axis=1, ti...  28.9 us
    dot_general x1, matrix products, local(): jnp.einsum('lrd,ldf->lrf', batch, weight_in, preferred_element_type=jnp.f...  5.32 us
    dot_general x1, matrix products, local(): jnp.einsum('lrf,lfd->lrd', hidden, weight_out, preferred_element_type=jnp...  5.1 us

commit v1 on v0

--- a/solution.py
+++ b/solution.py
@@ -42,7 +42,10 @@
         "lrf,lfd->lrd", hidden, weight_out, preferred_element_type=jnp.float32
     ).astype(jnp.bfloat16)
     shaped_back = result.reshape(local_experts, devices_all, capacity, width)
-    returned = lax.all_to_all(shaped_back, ("ex", "ey"), split_axis=1, concat_axis=1, tiled=True)
+    devices = lax.axis_size(("ex", "ey"))
+    blocks = jnp.stack(jnp.split(shaped_back, devices, axis=1), axis=0)
+    blocks = lax.all_to_all(blocks, ("ex", "ey"), split_axis=0, concat_axis=0)
+    returned = jnp.concatenate(blocks, axis=1)
     back_rows = returned.reshape(groups * capacity, width)
     gathered = jnp.einsum("rt,rd->td", placing, back_rows, preferred_element_type=jnp.float32)
     return (gathered * probability[:, None]).astype(jnp.bfloat16)

time: 84.6 us -> 92.4 us (1.092)
  matrix products: 12.7 us -> 19.1 us
    dot_general x1, matrix products: 5.32 us -> 9.08 us  [local(): jnp.einsum('lrd,ldf->lrf', batch, weight_in, preferred_element_type=jnp.f...]
    dot_general x1, matrix products: 5.1 us -> 7.77 us  [local(): jnp.einsum('lrf,lfd->lrd', hidden, weight_out, preferred_element_type=jnp...]
    unnamed x12 -> x131, local copies, waits for them, and re-layouts: 0.3 us -> 2 us
where the time goes in v1:
time: 92.4 us; the launch traced here: 92.2 us
  blocking collectives  65.1 us (70%)
  matrix products  19.1 us (21%)
  local copies, waits for them, and re-layouts  5.24 us (6%)
  other arithmetic  2.1 us (2%)
    all_to_all x1, blocking collectives, local(): lax.all_to_all(shaped, ('ex', 'ey'), split_axis=1, concat_axis=1, tiled=T...  36.2 us
    all_to_all x1, blocking collectives, local(): blocks = lax.all_to_all(blocks, ('ex', 'ey'), split_axis=0, concat_axis=0)  28.9 us
    dot_general x1, matrix products, local(): jnp.einsum('lrd,ldf->lrf', batch, weight_in, preferred_element_type=jnp.f...  9.08 us
    dot_general x1, matrix products, local(): jnp.einsum('lrf,lfd->lrd', hidden, weight_out, preferred_element_type=jnp...  7.77 us
    unnamed x131, local copies, waits for them, and re-layouts  2 us

profile of v1, /device:TPU:1, one launch (start us, length us, event | category | flops | bytes accessed | tf_op | source)
XLA Modules:
  0.0 92.2 jit_solution(16543388121818346777)
XLA Ops:
  0.0 0.0 copy-start
  0.0 0.7 broadcast_multiply_fusion.1
  0.7 0.7 add.10
  1.4 0.3 fusion.1
  1.7 0.7 convert_add_fusion
  2.4 0.0 copy-done
  2.4 0.6 convolution_convert_fusion.1
  3.0 0.4 reshape.19
  3.4 0.5 copy.262
  3.9 36.2 %all_to_all.10 = bf16[2,128,4,768]{3,2,0,1:T(4,128)(2,1)S(1)} all-to-all(bf16[2,128,4,768]{3,2,0,1:T(4,128)(2,1)S(1)} %copy.262), channel_id=1, replica_groups=mesh['ex'=16,'ey'=8] {'ex','ey'}, dimensions={1} | all-to-all | bytes 3145728 | tf_op jit(solution)/shard_map/all_to_all | solution.py:34
  40.2 0.5 copy.263
  40.7 0.4 reshape.20
  41.1 9.1 %maximum_convert_fusion = bf16[2,512,3072]{2,1,0:T(8,128)(2,1)S(1)} fusion(bf16[2,512,768]{2,1,0:T(8,128)(2,1)S(1)} %reshape.20, bf16[2,768,3072]{2,1,0:T(8,128)(2,1)} %param.10), kind=kOutput, calls=%fused_computation | convolution fusion | flops 4838129664 | bytes 17301504 | tf_op jit(solution)/shard_map/lrd,ldf->lrf/dot_general | solution.py:39
  50.2 7.8 %convolution_convert_fusion = bf16[2,512,768]{2,1,0:T(8,128)(2,1)S(1)} fusion(bf16[2,512,3072]{2,1,0:T(8,128)(2,1)S(1)} %maximum_convert_fusion, bf16[2,3072,768]{2,1,0:T(8,128)(2,1)} %param.11), kind=kOutput, calls=%fused_computation.1 | convolution fusion | flops 4832624640 | bytes 17301504 | tf_op jit(solution)/shard_map/lrf,lfd->lrd/dot_general | solution.py:41
  58.0 0.4 reshape.21
  60.7 28.9 %all_to_all.11 = bf16[128,2,1,4,768]{4,3,1,2,0:T(4,128)(2,1)S(1)} all-to-all(bf16[128,2,1,4,768]{4,3,1,2,0:T(4,128)(2,1)S(1)} %constant_dynamic-update-slice_fusion), channel_id=1, replica_groups=mesh['ex'=16,'ey'=8] {'ex','ey'}, dimensions={0} | all-to-all | bytes 3145728 | tf_op jit(solution)/shard_map/all_to_all | solution.py:47
  89.5 0.5 copy.392
  90.1 0.0 copy-start.1
  90.1 0.4 reshape_reshape.3
  90.5 0.3 copy-done.1
  90.8 1.4 %fusion = bf16[256,768]{1,0:T(8,128)(2,1)} fusion(bf16[1024,768]{1,0:T(8,128)(2,1)S(1)} %reshape_reshape.3, s32[256]{0:T(256)S(1)} %convert_add_fusion, f32[256]{0:T(256)S(1)} %copy-done.1), kind=kOutput, calls=%fused_computation.4 | convolution fusion | flops 403308544 | bytes 1968128 | tf_op jit(solution)/shard_map/rt,rd->td/dot_general | solution.py:50
  (128 shorter events, 1.7 us)
Async XLA Ops:
  0.0 2.4 %copy-start = (bf16[256,768]{1,0:T(8,128)(2,1)S(1)}, bf16[256,768]{1,0:T(8,128)(2,1)}, u32[]{:S(2)}) copy-start(bf16[256,768]{1,0:T(8,128)(2,1)} %param.6) | copy-start | bytes 1179652
  90.1 0.7 copy-start.1
